TPU v7x, 128 devices: a whole 4x4x4 slice. The times are simulated.
128 devices in a mesh: row: 16 (over y, z), col: 8 (over x, core).
Axes of the slice: x: 4, y: 4, z: 4, core: 2. Of those that a mesh axis runs over, the one named last changes fastest.
Arguments:
- kernel_rows: float32 [2, 16, 8, 64, 16384], P(None, 'row', 'col'), may hold values from -1 to 8, as said below
Outputs:
- factored: float32 [2, 16, 512, 4, 8, 512], P(None, 'row', None, None, 'col')
Inputs may be any that keep to these rules, and one draw needn't show every extreme that they name: `kernel_rows`: the matrix A that the rows make is symmetric and positive definite.
All inputs are finite; a program needn't handle non-finite values.
Results may differ from a plain program's by a relative error of at most 0.0001.
Values sent between devices are 32-bit elements; how exact they have to be, the bound alone decides.
A program may use at most 128 MiB of HBM per device.

v0:
```python
import jax
import jax.numpy as jnp
from jax import lax
from jax.sharding import PartitionSpec as P


def spread(block, axis, owner):
    block = jnp.where(lax.axis_index(axis) == owner, block, jnp.zeros_like(block))
    return lax.psum(block, axis)


def solve_rows(factor_tile, column):
    row_tiles, tile_size = (column.shape[0], column.shape[1])
    stacked = column.reshape(row_tiles * tile_size, tile_size)
    solved = jax.scipy.linalg.solve_triangular(factor_tile, stacked.T, lower=True)
    return solved.T.reshape(row_tiles, tile_size, tile_size)


def factor(tiles_here, panel_idx, grid_rows, grid_cols):
    row_at, col_at = (panel_idx // grid_rows, panel_idx // grid_cols)
    row_root, col_root = (panel_idx % grid_rows, panel_idx % grid_cols)
    column = tiles_here[:, :, col_at, :]
    diag_piece = tiles_here[row_at, :, col_at, :]
    diag_tile = spread(diag_piece, "row", row_root)
    factor_tile = jnp.linalg.cholesky(diag_tile)
    solved = spread(solve_rows(factor_tile, column), "col", col_root)
    return (factor_tile, solved)


def mirror(solved, grid_rows, grid_cols):
    pieces = []
    for copy_idx in range(grid_rows // grid_cols):
        root_row = lax.axis_index("col") + copy_idx * grid_cols
        pieces.append(spread(solved, "row", root_row))
    row_tiles, tile_size = (solved.shape[0], solved.shape[1])
    return jnp.stack(pieces, axis=1).reshape(-1, tile_size, tile_size)


def update(
    tiles_here, panel_idx, factor_tile, solved, col_factor, row_ids, col_ids, grid_rows, grid_cols
):
    left_part = jnp.where((row_ids > panel_idx)[:, None, None], solved, jnp.float32(0.0))
    right_part = jnp.where((col_ids > panel_idx)[:, None, None], col_factor, jnp.float32(0.0))
    tiles_here = tiles_here - jnp.einsum(
        "aur,bvr->aubv", left_part, right_part, precision=lax.Precision.HIGHEST
    )
    row_at, col_at = (panel_idx // grid_rows, panel_idx // grid_cols)
    row_root, col_root = (panel_idx % grid_rows, panel_idx % grid_cols)
    below_mask = (row_ids > panel_idx)[:, None, None]
    diag_mask = (row_ids == panel_idx)[:, None, None]
    col_values = jnp.where(
        below_mask, solved, jnp.where(diag_mask, factor_tile[None], jnp.float32(0.0))
    )
    owner_col = lax.axis_index("col") == col_root
    tiles_here = tiles_here.at[:, :, col_at, :].set(
        jnp.where(owner_col, col_values, tiles_here[:, :, col_at, :])
    )
    zero_mask = (lax.axis_index("row") == row_root) & (col_ids > panel_idx)
    tiles_here = tiles_here.at[row_at].set(
        jnp.where(zero_mask[None, :, None], jnp.float32(0.0), tiles_here[row_at])
    )
    return tiles_here


def shards(kernel_rows):
    grid_rows = lax.axis_size("row")
    grid_cols = lax.axis_size("col")
    row_tiles, sub_rows, mat_order = (
        kernel_rows.shape[0],
        kernel_rows.shape[3],
        kernel_rows.shape[4],
    )
    tile_size = sub_rows * grid_cols
    col_tiles = mat_order // (tile_size * grid_cols)
    shaped = kernel_rows.reshape(row_tiles, sub_rows, col_tiles, grid_cols, tile_size)
    placed = lax.all_to_all(shaped, "col", split_axis=3, concat_axis=1, tiled=True)
    tiles_here = placed.reshape(row_tiles, tile_size, col_tiles, tile_size)
    row_ids = jnp.arange(row_tiles, dtype=jnp.int32) * grid_rows + lax.axis_index("row")
    col_ids = jnp.arange(col_tiles, dtype=jnp.int32) * grid_cols + lax.axis_index("col")
    for panel_idx in range(2):
        factor_tile, solved = factor(tiles_here, panel_idx, grid_rows, grid_cols)
        col_factor = mirror(solved, grid_rows, grid_cols)
        tiles_here = update(
            tiles_here,
            panel_idx,
            factor_tile,
            solved,
            col_factor,
            row_ids,
            col_ids,
            grid_rows,
            grid_cols,
        )
    return tiles_here.reshape(row_tiles, 1, tile_size, col_tiles, 1, tile_size)


def solution(mesh):
    return jax.shard_map(
        shards,
        mesh=mesh,
        in_specs=(P(None, "row", "col", None, None),),
        out_specs=P(None, "row", None, None, "col", None),
        check_vma=False,
    )
```

profile of v0, /device:TPU:1, one launch (start us, length us, event | category | flops | bytes accessed | tf_op | source)
XLA Modules:
  0.0 1100.3 jit_solution(1424373501177448121)
XLA Ops:
  6.5 13.3 %copy.99 = f32[16,8,32,512]{3,2,1,0:T(8,128)} copy(f32[16,8,32,512]{3,1,2,0:T(8,128)} %bitcast.198) | data formatting | bytes 16777216
  19.8 23.6 %copy.63 = f32[2,64,4,8,512]{4,2,1,0,3:T(4,128)} copy(f32[2,64,4,8,512]{4,3,2,1,0:T(8,128)} %bitcast.197) | data formatting | bytes 16777216 | tf_op jit(solution)/shard_map/reshape | solution.py:75
  49.6 93.7 %all-to-all-done = f32[2,64,4,8,512]{4,2,1,0,3:T(4,128)} async-done(((f32[2,64,4,8,512]{4,2,1,0,3:T(4,128)}), f32[2,64,4,8,512]{4,2,1,0,3:T(4,128)}, u32[]{:S(2)}, u32[]{:S(2)}) %all-to-all-start) | async-done | bytes 8388640 | tf_op jit(solution)/shard_map/all_to_all | solution.py:76
  159.2 82.0 %all-reduce.10.cloned.1.call-done = f32[512,512]{0,1:T(8,128)} async-done(((f32[512,512]{0,1:T(8,128)}), f32[512,512]{0,1:T(8,128)}) %all-reduce.10.cloned.1.call-update) | async-done | bytes 1048592 | tf_op jit(solution)/shard_map/psum | solution.py:9
  246.3 11.7 %cholesky.286 = f32[128,128]{1,0:T(8,128)S(1)} custom-call(f32[128,128]{1,0:T(8,128)S(1)} %cholesky.426), custom_call_target="Cholesky" | custom-call | tf_op jit(solution)/shard_map/jit(cholesky)/cholesky | solution.py:25
  270.6 11.7 %cholesky.305 = f32[128,128]{1,0:T(8,128)S(1)} custom-call(f32[128,128]{1,0:T(8,128)S(1)} %cholesky.430), custom_call_target="Cholesky" | custom-call | tf_op jit(solution)/shard_map/jit(cholesky)/cholesky | solution.py:25
  294.1 11.7 %cholesky.326 = f32[128,128]{1,0:T(8,128)S(1)} custom-call(f32[128,128]{1,0:T(8,128)S(1)} %cholesky.435), custom_call_target="Cholesky" | custom-call | tf_op jit(solution)/shard_map/jit(cholesky)/cholesky | solution.py:25
  317.8 11.7 %cholesky.343 = f32[128,128]{1,0:T(8,128)S(1)} custom-call(f32[128,128]{1,0:T(8,128)S(1)} %convolution_subtract_fusion.9), custom_call_target="Cholesky" | custom-call | tf_op jit(solution)/shard_map/jit(cholesky)/cholesky | solution.py:25
  335.3 11.7 %while.8 = (s32[]{:T(128)}, f32[512,512]{1,0:T(8,128)}, s32[4,2]{0,1:T(2,128)S(1)}, f32[4,128,128]{2,1,0:T(8,128)S(1)}, s32[]{:T(128)}) while((s32[]{:T(128)}, f32[512,512]{1,0:T(8,128)}, s32[4,2]{0,1:T(2,128)S(1)}, f32[4,128,128]{2,1,0:T(8,128)S(1)}, s32[]{:T(128)}) %tuple.74), condition=%wide.while_cond.4, body=%wide.while_body.4.sunk | while | flops 2 | bytes 131181 | solution.py:15
  347.0 39.3 %custom-call.30 = f32[4,128,128]{1,2,0:T(8,128)S(1)} custom-call(f32[4,128,128]{2,1,0:T(8,128)S(1)} %get-tuple-element.69), custom_call_target="InvertDiagBlocksLowerTriangular" | custom-call | tf_op jit(solution)/shard_map/jit(_solve_triangular)/triangular_solve | solution.py:15
  399.0 64.5 %all-reduce.12.cloned.1.call-done = f32[2,512,512]{1,2,0:T(8,128)} async-done(((f32[2,512,512]{1,2,0:T(8,128)}), f32[2,512,512]{1,2,0:T(8,128)}) %all-reduce.12.cloned.1.call-update) | async-done | bytes 2097168 | tf_op jit(solution)/shard_map/psum | solution.py:9
  478.4 94.4 %all-reduce.20.cloned.1.call-done = (f32[2,1,512,512]{2,3,0,1:T(8,128)}, f32[2,1,512,512]{2,3,0,1:T(8,128)}) async-done(((f32[2,1,512,512]{2,3,0,1:T(8,128)}, f32[2,1,512,512]{2,3,0,1:T(8,128)}), (f32[2,1,512,512]{2,3,0,1:T(8,128)}, f32[2,1,512,512]{2,3,0,1:T(8,128)})) %all-reduce.20.cloned.1.call-update) | async-done | bytes 4194320 | tf_op jit(solution)/shard_map/psum | solution.py:9
  585.9 18.0 %fusion.10 = f32[2,512,4,512]{1,3,0,2:T(8,128)S(1)} fusion(f32[2,512,4,512]{1,3,0,2:T(8,128)} %copy.72, f32[4,512,512]{2,1,0:T(8,128)S(1)} %bitcast_select_fusion.1, f32[2,512,512]{1,2,0:T(8,128)S(1)} %copy-done.1, pred[2]{0:T(512)(128)(4,1)S(1)} %get-tuple-element.130), kind=kOutput, calls=%fused_computation.18 | convolution fusion | flops 12887523328 | bytes 23068674 | tf_op jit(solution)/shard_map/aur,bvr->aubv/dot_general | solution.py:44
  622.5 80.2 %all-reduce.14.cloned.1.call-done = f32[512,512]{0,1:T(8,128)} async-done(((f32[512,512]{0,1:T(8,128)}), f32[512,512]{0,1:T(8,128)}) %all-reduce.14.cloned.1.call-update) | async-done | bytes 1048592 | tf_op jit(solution)/shard_map/psum | solution.py:9
  707.9 11.7 %cholesky.358 = f32[128,128]{1,0:T(8,128)S(1)} custom-call(f32[128,128]{1,0:T(8,128)S(1)} %cholesky.439), custom_call_target="Cholesky" | custom-call | tf_op jit(solution)/shard_map/jit(cholesky)/cholesky | solution.py:25
  732.1 11.7 %cholesky.377 = f32[128,128]{1,0:T(8,128)S(1)} custom-call(f32[128,128]{1,0:T(8,128)S(1)} %cholesky.443), custom_call_target="Cholesky" | custom-call | tf_op jit(solution)/shard_map/jit(cholesky)/cholesky | solution.py:25
  756.7 11.7 %cholesky.398 = f32[128,128]{1,0:T(8,128)S(1)} custom-call(f32[128,128]{1,0:T(8,128)S(1)} %cholesky.448), custom_call_target="Cholesky" | custom-call | tf_op jit(solution)/shard_map/jit(cholesky)/cholesky | solution.py:25
  780.4 11.7 %cholesky.415 = f32[128,128]{1,0:T(8,128)S(1)} custom-call(f32[128,128]{1,0:T(8,128)S(1)} %convolution_subtract_fusion.8), custom_call_target="Cholesky" | custom-call | tf_op jit(solution)/shard_map/jit(cholesky)/cholesky | solution.py:25
  797.2 11.7 %while.9 = (s32[]{:T(128)}, f32[512,512]{1,0:T(8,128)}, s32[4,2]{0,1:T(2,128)S(1)}, f32[4,128,128]{2,1,0:T(8,128)S(1)}, s32[]{:T(128)}) while((s32[]{:T(128)}, f32[512,512]{1,0:T(8,128)}, s32[4,2]{0,1:T(2,128)S(1)}, f32[4,128,128]{2,1,0:T(8,128)S(1)}, s32[]{:T(128)}) %tuple.94), condition=%wide.while_cond.4.clone, body=%wide.while_body.4.clone.sunk | while | flops 2 | bytes 131181 | solution.py:15
  809.0 39.3 %custom-call.34 = f32[4,128,128]{1,2,0:T(8,128)S(1)} custom-call(f32[4,128,128]{2,1,0:T(8,128)S(1)} %get-tuple-element.70), custom_call_target="InvertDiagBlocksLowerTriangular" | custom-call | tf_op jit(solution)/shard_map/jit(_solve_triangular)/triangular_solve | solution.py:15
  861.0 64.4 %all-reduce.16.cloned.1.call-done = f32[2,512,512]{1,2,0:T(8,128)} async-done(((f32[2,512,512]{1,2,0:T(8,128)}), f32[2,512,512]{1,2,0:T(8,128)}) %all-reduce.16.cloned.1.call-update) | async-done | bytes 2097168 | tf_op jit(solution)/shard_map/psum | solution.py:9
  931.2 103.5 %all-reduce.18.cloned.1.call-done = (f32[2,1,512,512]{2,3,0,1:T(8,128)}, f32[2,1,512,512]{2,3,0,1:T(8,128)}) async-done(((f32[2,1,512,512]{2,3,0,1:T(8,128)}, f32[2,1,512,512]{2,3,0,1:T(8,128)}), (f32[2,1,512,512]{2,3,0,1:T(8,128)}, f32[2,1,512,512]{2,3,0,1:T(8,128)})) %all-reduce.18.cloned.1.call-update) | async-done | bytes 4194320 | tf_op jit(solution)/shard_map/psum | solution.py:9
  1047.9 18.0 %fusion.7 = f32[2,512,4,512]{1,3,2,0:T(8,128)S(1)} fusion(f32[2,512,4,512]{1,3,2,0:T(8,128)} %get-tuple-element.93, f32[4,512,512]{2,1,0:T(8,128)S(1)} %bitcast_select_fusion, f32[2,512,512]{1,2,0:T(8,128)S(1)} %copy-done.2, pred[2]{0:T(512)(128)(4,1)S(1)} %get-tuple-element.132), kind=kOutput, calls=%fused_computation.17 | convolution fusion | flops 12887523328 | bytes 23068674 | tf_op jit(solution)/shard_map/aur,bvr->aubv/dot_general | solution.py:44
  1072.5 20.5 %copy.88 = f32[2,1,512,4,1,512]{5,4,3,2,1,0:T(1,128)} copy(f32[2,1,512,4,1,512]{2,5,3,0,4,1:T(8,128)} %fusion.2) | data formatting | bytes 16777216 | tf_op jit(solution)/shard_map/scatter | solution.py:59
  (159 shorter events, 231.9 us)
Async XLA Ops:
  43.4 100.0 %all-to-all-start = ((f32[2,64,4,8,512]{4,2,1,0,3:T(4,128)}), f32[2,64,4,8,512]{4,2,1,0,3:T(4,128)}, u32[]{:S(2)}, u32[]{:S(2)}) async-start(f32[2,64,4,8,512]{4,2,1,0,3:T(4,128)} %copy.63), calls=%async_computation | async-start | bytes 16777216 | tf_op jit(solution)/shard_map/all_to_all | solution.py:76
  49.6 191.6 %all-reduce.10.cloned.1.call-start = ((), (), s32[]{:S(2)}) async-start(), calls=%async_computation.1 | async-start | bytes 2097152 | tf_op jit(solution)/shard_map/psum | solution.py:9
  149.2 3.4 copy-start
  154.1 309.3 %all-reduce.12.cloned.1.call-start = ((), (), s32[]{:S(2)}) async-start(), calls=%async_computation.2 | async-start | bytes 4194304 | tf_op jit(solution)/shard_map/psum | solution.py:9
  241.2 2.6 copy-start.3
  245.3 1.0 copy-start.8
  398.9 173.9 %all-reduce.20.cloned.1.call-start = ((), (), s32[]{:S(2)}) async-start(), calls=%async_computation.6 | async-start | bytes 8388608 | tf_op jit(solution)/shard_map/psum | solution.py:9
  467.8 235.0 %all-reduce.14.cloned.1.call-start = ((), (), s32[]{:S(2)}) async-start(), calls=%async_computation.3 | async-start | bytes 2097152 | tf_op jit(solution)/shard_map/psum | solution.py:9
  467.9 10.2 copy-start.5
  582.7 3.2 copy-start.1
  616.4 309.0 %all-reduce.16.cloned.1.call-start = ((), (), s32[]{:S(2)}) async-start(), calls=%async_computation.4 | async-start | bytes 4194304 | tf_op jit(solution)/shard_map/psum | solution.py:9
  702.8 2.6 copy-start.4
  706.8 1.0 copy-start.7
  860.9 173.8 %all-reduce.18.cloned.1.call-start = ((), (), s32[]{:S(2)}) async-start(), calls=%async_computation.5 | async-start | bytes 8388608 | tf_op jit(solution)/shard_map/psum | solution.py:9
  929.6 1.2 copy-start.6
  1044.7 3.2 copy-start.2
Sparse Core Ops, SparseCore 0:
  154.2 86.9 all-reduce.9
  399.0 64.3 all-reduce.11
  467.9 104.8 all-reduce.19
  616.5 86.1 all-reduce.13
  861.0 64.2 all-reduce.15
  929.8 104.8 all-reduce.17
where the time goes:
time: 1110 us; the launch traced here: 1100 us
  waiting for transfers between devices  583 us (53%)
  other arithmetic  280 us (25%)
  local copies, waits for them, and re-layouts  149 us (13%)
  matrix products  62.2 us (6%)
  between operations  19.6 us (2%)
    psum x6, waiting for transfers between devices, spread(): return lax.psum(block, axis)  489 us
    another operation x29, other arithmetic, factor(): factor_tile = jnp.linalg.cholesky(diag_tile)  158 us
    all_to_all x1, waiting for transfers between devices, shards(): lax.all_to_all(shaped, 'col', split_axis=3, concat_axis=1, tiled=True)  93.7 us
    another operation x5, other arithmetic, solve_rows(): jax.scipy.linalg.solve_triangular(factor_tile, stacked.T, lower=True)  82.2 us
    dot_general x2, matrix products, update(): jnp.einsum('aur,bvr->aubv', left_part, right_part, precision=lax.Precisio...  36 us
    reshape x1, local copies, waits for them, and re-layouts, shards(): kernel_rows.reshape(row_tiles, sub_rows, col_tiles, grid_cols, tile_size)  23.6 us
    unnamed x21, local copies, waits for them, and re-layouts  23.4 us
    another operation x27, local copies, waits for them, and re-layouts, solve_rows(): jax.scipy.linalg.solve_triangular(factor_tile, stacked.T, lower=True)  23.3 us
  transfers between devices with their start and end apart: 7, of which 7 were waited for; matrix products, arithmetic and copies ran while one was open for 2% of the time, Pallas kernels for 0%

commit v1 on v0

--- a/solution.py
+++ b/solution.py
@@ -3,10 +3,12 @@
 from jax import lax
 from jax.sharding import PartitionSpec as P
 
+render_keys = lambda slab_in, row_axis: jnp.sum(lax.all_gather(slab_in, row_axis), 0)
+
 
 def spread(block, axis, owner):
     block = jnp.where(lax.axis_index(axis) == owner, block, jnp.zeros_like(block))
-    return lax.psum(block, axis)
+    return render_keys(block, axis)
 
 
 def solve_rows(factor_tile, column):

time: 1110 us -> 1820 us (1.64)
  waiting for transfers between devices: 583 us -> 1230 us
  other arithmetic: 280 us -> 362 us
  local copies, waits for them, and re-layouts: 149 us -> 106 us
  matrix products: 62.2 us -> 88 us
    all_gather x0 -> x8, waiting for transfers between devices: none -> 1140 us  [lax.all_gather(slab_in, row_axis)]
    psum x6 -> x0, waiting for transfers between devices: 489 us -> none  [spread(): return lax.psum(block, axis)]
    reduce_sum x0 -> x8, other arithmetic: none -> 89.3 us  [jnp.sum(lax.all_gather(slab_in, row_axis), 0)]
    dot_general x2, matrix products: 36 us -> 61.8 us  [update(): jnp.einsum('aur,bvr->aubv', left_part, right_part, precision=lax.Precisio...]
  transfers between devices with their start and end apart: 7 -> 9, of which waited for: 7 -> 9; matrix products, arithmetic and copies ran while one was open for 2% -> 3% of each run, Pallas kernels for 0% -> 0%
where the time goes in v1:
time: 1820 us; the launch traced here: 1810 us
  waiting for transfers between devices  1230 us (68%)
  other arithmetic  362 us (20%)
  local copies, waits for them, and re-layouts  106 us (6%)
  matrix products  88 us (5%)
  between operations  19.7 us (1%)
    all_gather x8, waiting for transfers between devices, lax.all_gather(slab_in, row_axis)  1140 us
    another operation x29, other arithmetic, factor(): factor_tile = jnp.linalg.cholesky(diag_tile)  159 us
    all_to_all x1, waiting for transfers between devices, shards(): lax.all_to_all(shaped, 'col', split_axis=3, concat_axis=1, tiled=True)  93.7 us
    reduce_sum x8, other arithmetic, jnp.sum(lax.all_gather(slab_in, row_axis), 0)  89.3 us
    another operation x5, other arithmetic, solve_rows(): jax.scipy.linalg.solve_triangular(factor_tile, stacked.T, lower=True)  81.8 us
    dot_general x2, matrix products, update(): jnp.einsum('aur,bvr->aubv', left_part, right_part, precision=lax.Precisio...  61.8 us
  transfers between devices with their start and end apart: 9, of which 9 were waited for; matrix products, arithmetic and copies ran while one was open for 3% of the time, Pallas kernels for 0%

profile of v1, /device:TPU:1, one launch (start us, length us, event | category | flops | bytes accessed | tf_op | source)
XLA Modules:
  0.0 1814.3 jit_solution(13033943822335481092)
XLA Ops:
  31.1 93.7 %all-to-all-done = f32[2,64,4,8,512]{4,1,2,0,3:T(8,128)} async-done(((f32[2,64,4,8,512]{4,1,2,0,3:T(8,128)}), f32[2,64,4,8,512]{4,1,2,0,3:T(8,128)}, u32[]{:S(2)}, u32[]{:S(2)}) %all-to-all-start) | async-done | bytes 8388640 | tf_op jit(solution)/shard_map/all_to_all | solution.py:78
  138.9 107.1 %all-gather.19.cloned.1.call-done = f32[16,512,1,512]{3,1,2,0:T(8,128)} async-done(((f32[1,512,1,512]{3,1,2,0:T(8,128)}), f32[16,512,1,512]{3,1,2,0:T(8,128)}) %all-gather.19.cloned.1.call-update) | async-done | bytes 16777232 | tf_op jit(solution)/shard_map/all_gather | solution.py:6
  257.7 11.7 cholesky.286
  281.9 12.1 cholesky.305
  305.4 11.7 cholesky.326
  329.1 11.9 cholesky.343
  358.3 39.3 %custom-call.30 = f32[4,128,128]{1,2,0:T(8,128)S(1)} custom-call(f32[4,128,128]{2,1,0:T(8,128)S(1)} %get-tuple-element.69), custom_call_target="InvertDiagBlocksLowerTriangular" | custom-call | tf_op jit(solution)/shard_map/jit(_solve_triangular)/triangular_solve | solution.py:17
  407.5 85.1 %all-gather.15.cloned.1.call-done = f32[8,2,512,512]{3,2,1,0:T(8,128)} async-done(((f32[1,2,512,512]{3,2,1,0:T(8,128)}), f32[8,2,512,512]{3,2,1,0:T(8,128)}) %all-gather.15.cloned.1.call-update) | async-done | bytes 16777232 | tf_op jit(solution)/shard_map/all_gather | solution.py:6
  516.5 193.0 %all-gather.21.cloned.1.call-done = f32[32,512,512]{2,1,0:T(8,128)} async-done(((f32[2,512,512]{2,1,0:T(8,128)}), f32[32,512,512]{2,1,0:T(8,128)}) %all-gather.21.cloned.1.call-update) | async-done | bytes 33554448 | tf_op jit(solution)/shard_map/all_gather | solution.py:6
  709.5 14.6 reduce_sum.78
  724.1 184.1 %all-gather.23.cloned.1.call-done = f32[32,512,512]{2,1,0:T(8,128)} async-done(((f32[2,512,512]{2,1,0:T(8,128)}), f32[32,512,512]{2,1,0:T(8,128)}) %all-gather.23.cloned.1.call-update) | async-done | bytes 33554448 | tf_op jit(solution)/shard_map/all_gather | solution.py:6
  908.2 14.1 reduce_sum.79
  928.1 29.1 %fusion.7 = f32[2,512,4,512]{3,1,2,0:T(8,128)} fusion(f32[2,512,4,512]{3,1,2,0:T(8,128)S(1)} %bitcast.167, f32[4,512,512]{2,1,0:T(8,128)S(1)} %bitcast_select_fusion.1, f32[2,512,512,1]{1,0,2,3:T(2,128)S(1)} %copy-done.2), kind=kOutput, calls=%fused_computation.17 | convolution fusion | flops 12886999040 | bytes 23068672 | tf_op jit(solution)/shard_map/aur,bvr->aubv/dot_general | solution.py:46
  971.9 106.0 %all-gather.25.cloned.1.call-done = f32[16,512,1,512]{3,1,2,0:T(8,128)} async-done(((f32[1,512,1,512]{3,1,2,0:T(8,128)}), f32[16,512,1,512]{3,1,2,0:T(8,128)}) %all-gather.25.cloned.1.call-update) | async-done | bytes 16777232 | tf_op jit(solution)/shard_map/all_gather | solution.py:6
  1113.8 12.1 cholesky.377
  1162.3 11.9 cholesky.415
  1190.8 39.3 %custom-call.34 = f32[4,128,128]{1,2,0:T(8,128)S(1)} custom-call(f32[4,128,128]{2,1,0:T(8,128)S(1)} %get-tuple-element.70), custom_call_target="InvertDiagBlocksLowerTriangular" | custom-call | tf_op jit(solution)/shard_map/jit(_solve_triangular)/triangular_solve | solution.py:17
  1240.0 85.1 %all-gather.17.cloned.1.call-done = f32[8,2,512,512]{3,2,1,0:T(8,128)} async-done(((f32[1,2,512,512]{3,2,1,0:T(8,128)}), f32[8,2,512,512]{3,2,1,0:T(8,128)}) %all-gather.17.cloned.1.call-update) | async-done | bytes 16777232 | tf_op jit(solution)/shard_map/all_gather | solution.py:6
  1348.9 193.1 %all-gather.27.cloned.1.call-done = f32[32,512,512]{2,1,0:T(8,128)} async-done(((f32[2,512,512]{2,1,0:T(8,128)}), f32[32,512,512]{2,1,0:T(8,128)}) %all-gather.27.cloned.1.call-update) | async-done | bytes 33554448 | tf_op jit(solution)/shard_map/all_gather | solution.py:6
  1542.0 14.5 reduce_sum.83
  1556.5 184.3 %all-gather.29.cloned.1.call-done = f32[32,512,512]{2,1,0:T(8,128)} async-done(((f32[2,512,512]{2,1,0:T(8,128)}), f32[32,512,512]{2,1,0:T(8,128)}) %all-gather.29.cloned.1.call-update) | async-done | bytes 33554448 | tf_op jit(solution)/shard_map/all_gather | solution.py:6
  1740.9 14.1 reduce_sum.84
  1759.2 32.7 %fusion.10 = f32[2,512,4,512]{3,1,2,0:T(8,128)S(1)} fusion(f32[2,512,4,512]{3,1,2,0:T(8,128)} %get-tuple-element.89, f32[4,512,512]{2,1,0:T(8,128)S(1)} %bitcast_select_fusion, f32[2,512,512,1]{1,0,2,3:T(2,128)S(1)} %copy-done.1), kind=kOutput, calls=%fused_computation.18 | convolution fusion | flops 12886999040 | bytes 23068672 | tf_op jit(solution)/shard_map/aur,bvr->aubv/dot_general | solution.py:46
  1794.3 12.7 copy.44
  (169 shorter events, 304.5 us)
Async XLA Ops:
  24.7 100.1 %all-to-all-start = ((f32[2,64,4,8,512]{4,1,2,0,3:T(8,128)}), f32[2,64,4,8,512]{4,1,2,0,3:T(8,128)}, u32[]{:S(2)}, u32[]{:S(2)}) async-start(f32[2,64,4,8,512]{4,1,2,0,3:T(8,128)} %copy.25), calls=%async_computation | async-start | bytes 16777216 | tf_op jit(solution)/shard_map/all_to_all | solution.py:78
  31.1 214.9 %all-gather.19.cloned.1.call-start = ((), (), s32[]{:S(2)}) async-start(), calls=%async_computation.3 | async-start | bytes 17825792 | tf_op jit(solution)/shard_map/all_gather | solution.py:6
  129.3 3.4 copy-start
  133.8 358.8 %all-gather.15.cloned.1.call-start = ((), (), s32[]{:S(2)}) async-start(), calls=%async_computation.1 | async-start | bytes 18874368 | tf_op jit(solution)/shard_map/all_gather | solution.py:6
  256.7 1.0 copy-start.6
  407.4 302.1 %all-gather.21.cloned.1.call-start = ((), (), s32[]{:S(2)}) async-start(), calls=%async_computation.4 | async-start | bytes 35651584 | tf_op jit(solution)/shard_map/all_gather | solution.py:6
  512.2 396.0 %all-gather.23.cloned.1.call-start = ((), (), s32[]{:S(2)}) async-start(), calls=%async_computation.5 | async-start | bytes 35651584 | tf_op jit(solution)/shard_map/all_gather | solution.py:6
  516.4 561.4 %all-gather.25.cloned.1.call-start = ((), (), s32[]{:S(2)}) async-start(), calls=%async_computation.6 | async-start | bytes 17825792 | tf_op jit(solution)/shard_map/all_gather | solution.py:6
  922.3 3.5 slice-start
  925.1 2.3 slice-start.1
  925.1 2.9 copy-start.2
  928.1 29.1 %copy-start.3 = (f32[512,512]{1,0:T(8,128)S(1)}, f32[512,512]{1,0:T(8,128)}, u32[]{:S(2)}) copy-start(f32[512,512]{1,0:T(8,128)} %get-tuple-element.92) | copy-start | bytes 3145732
  966.8 358.3 %all-gather.17.cloned.1.call-start = ((), (), s32[]{:S(2)}) async-start(), calls=%async_computation.2 | async-start | bytes 18874368 | tf_op jit(solution)/shard_map/all_gather | solution.py:6
  1088.5 1.0 copy-start.5
  1239.9 302.1 %all-gather.27.cloned.1.call-start = ((), (), s32[]{:S(2)}) async-start(), calls=%async_computation.7 | async-start | bytes 35651584 | tf_op jit(solution)/shard_map/all_gather | solution.py:6
  1344.7 396.2 %all-gather.29.cloned.1.call-start = ((), (), s32[]{:S(2)}) async-start(), calls=%async_computation.8 | async-start | bytes 35651584 | tf_op jit(solution)/shard_map/all_gather | solution.py:6
  1757.6 1.6 copy-start.1
  1759.2 32.7 %copy-start.4 = (f32[512,512]{1,0:T(8,128)S(1)}, f32[512,512]{1,0:T(8,128)}, u32[]{:S(2)}) copy-start(f32[512,512]{1,0:T(8,128)} %get-tuple-element.88) | copy-start | bytes 3145732
Sparse Core Ops, SparseCore 0:
  133.9 112.0 all-gather.18
  407.5 84.9 all-gather.14
  512.3 197.1 all-gather.20
  711.5 196.6 all-gather.22
  966.9 110.8 all-gather.24
  1240.0 84.9 all-gather.16
  1344.8 197.1 all-gather.26
  1544.1 196.6 all-gather.28
